TPU v7x, 256 devices: a whole 4x4x8 slice. The times are simulated.
256 devices in a mesh: gx: 16 (over z, x_hi), gy: 16 (over y, x_lo, core).
Axes of the slice: x: 4 (x_hi: 2, x_lo: 2; x = x_hi * 2 + x_lo), y: 4, z: 8, core: 2. Of those that a mesh axis runs over, the one named last changes fastest.
Arguments:
- f_in: float32 [19, 16, 256, 2048], P(None, None, 'gx', 'gy')
- rotor_place: int32 [40, 3], replicated, may hold values from 0 to 15, as said below
- marker_cell: int32 [40, 8192], replicated, may hold values from 16384 to 2078527, as said below
- pitch_phase: int32 [40, 2], replicated, may hold values from 0 to 63
- blade_area: float32 [16, 16, 2, 8192], P('gx', 'gy'), may hold values from 0.3 to 1.2
- blade_twist: float32 [16, 16, 2, 8192], P('gx', 'gy'), may hold values from -0.6 to 0.6
- blade_speed: float32 [16, 16, 2, 8192], P('gx', 'gy'), may hold values from 1.5 to 3
- blade_angle: float32 [16, 16, 2, 8192], P('gx', 'gy'), may hold values from -3.14 to 3.14, as said below
- filt_in: float32 [16, 16, 2, 3, 8192], P('gx', 'gy'), may hold values from -1.5 to 1.5
Outputs:
- f_out: float32 [19, 16, 256, 2048], P(None, None, 'gx', 'gy')
- loads_out: float32 [16, 16, 2, 3, 8192], P('gx', 'gy')
- filt_out: float32 [16, 16, 2, 3, 8192], P('gx', 'gy')
Inputs may be any that keep to these rules, and one draw needn't show every extreme that they name: `rotor_place`: column 0 is a streamwise tile holding at most 3 rotors, some exactly 3; column 1 a plane 0 to 15; column 2 the owner's spanwise tile. Every streamwise tile holds 2 or more rotors; one owner holds at most 2 rotors, exactly 2 in every streamwise tile. `marker_cell`: all stencil cells of one rotor lie within two neighbouring spanwise tiles and within levels 0 to 15; a rotor's stencils may cover one or two tiles. `blade_angle`: azimuths in radians.
All inputs are finite; a program needn't handle non-finite values.
Results may differ from a plain program's by a relative error of at most 0.0003.
Values sent between devices are 32-bit elements; how exact they have to be, the bound alone decides.
A program may use at most 128 MiB of HBM per device.

v0:
```python
import math

import jax
import jax.numpy as jnp
import numpy as np
from jax import lax
from jax.sharding import PartitionSpec as P

PHASES = 64


LATTICE_DIRS = np.array(
    [
        [0, 0, 0],
        [1, 0, 0],
        [-1, 0, 0],
        [0, 1, 0],
        [0, -1, 0],
        [0, 0, 1],
        [0, 0, -1],
        [1, 1, 0],
        [-1, -1, 0],
        [1, -1, 0],
        [-1, 1, 0],
        [1, 0, 1],
        [-1, 0, -1],
        [1, 0, -1],
        [-1, 0, 1],
        [0, 1, 1],
        [0, -1, -1],
        [0, 1, -1],
        [0, -1, 1],
    ]
)
OPPOSITE = [0, 2, 1, 4, 3, 6, 5, 8, 7, 10, 9, 12, 11, 14, 13, 16, 15, 18, 17]
LATTICE_WEIGHTS = np.array([1.0 / 3.0] + [1.0 / 18.0] * 6 + [1.0 / 36.0] * 12)
OMEGA = 1.0 / 0.6
SPREAD = 0.01
MIX = 0.5
PITCH_AMP = 0.2


def extended(block, sides, width):
    for axis, dim in sides:
        count = lax.axis_size(axis)
        forward = [(i, i + 1) for i in range(count - 1)]
        forward.append((count - 1, 0))
        backward = [(target, source) for source, target in forward]
        low = lax.ppermute(
            lax.slice_in_dim(block, block.shape[dim] - width, None, axis=dim), axis, forward
        )
        high = lax.ppermute(lax.slice_in_dim(block, 0, width, axis=dim), axis, backward)
        block = jnp.concatenate([low, block, high], axis=dim)
    return block


def peskin(offsets):
    distance = jnp.abs(offsets)
    near_arg = jnp.maximum(1.0 + 4.0 * distance - 4.0 * distance * distance, 1.0)
    far_arg = jnp.maximum(-7.0 + 12.0 * distance - 4.0 * distance * distance, 1.0)
    near_part = (3.0 - 2.0 * distance + jnp.sqrt(near_arg)) / 8.0
    far_part = (5.0 - 2.0 * distance - jnp.sqrt(far_arg)) / 8.0
    return jnp.where(distance <= 1.0, near_part, far_part)


def dense_rows(anchor, weights, width, start):
    column = jnp.arange(width, dtype=jnp.int32)[None, :] + start
    gap = column - anchor[:, None]
    summed = jnp.zeros(gap.shape, jnp.float32)
    for corner in range(4):
        summed = summed + jnp.where(gap == corner, weights[corner][:, None], 0.0)
    return summed


def stencil_tables(cell_codes, levels, width, start):
    fraction_z = (cell_codes % 8).astype(jnp.float32) / 8.0
    fraction_y = (cell_codes // 8 % 8).astype(jnp.float32) / 8.0
    cell_z = cell_codes // 64 % levels
    cell_y = cell_codes // (64 * levels)
    weights_y = [peskin(corner - 1.0 - fraction_y) for corner in range(4)]
    weights_z = [peskin(corner - 1.0 - fraction_z) for corner in range(4)]
    across = dense_rows(cell_y, weights_y, width, start)
    upward = dense_rows(cell_z, weights_z, levels, jnp.int32(0))
    return (across, upward)


def sample_section(section, across, upward):
    levels = section.shape[1]
    width = section.shape[2]
    flattened = jnp.transpose(section, (2, 0, 1)).reshape(width, 3 * levels)
    partial_value = jnp.dot(
        across, flattened, precision=lax.Precision.HIGHEST, preferred_element_type=jnp.float32
    )
    partial_value = partial_value.reshape(across.shape[0], 3, levels)
    return jnp.transpose(jnp.sum(partial_value * upward[:, None, :], axis=2))


def spread_section(marker_loads, across, upward):
    markers = upward.shape[0]
    levels = upward.shape[1]
    weighted = (upward[:, None, :] * jnp.transpose(marker_loads)[:, :, None]).reshape(
        markers, 3 * levels
    )
    section = lax.dot_general(
        weighted,
        across,
        (((0,), (0,)), ((), ())),
        precision=lax.Precision.HIGHEST,
        preferred_element_type=jnp.float32,
    )
    return -SPREAD * section.reshape(3, levels, across.shape[1])


def pitch_angles(phases):
    return PITCH_AMP * jnp.sin(2.0 * math.pi * phases.astype(jnp.float32) / PHASES)


def blade_loads(filtered, area, twist, speed, angle, pitch):
    axial_speed = filtered[..., 0, :]
    sin_t = jnp.sin(angle)
    cos_t = jnp.cos(angle)
    tangent = speed + sin_t * filtered[..., 1, :] - cos_t * filtered[..., 2, :]
    square = axial_speed * axial_speed + tangent * tangent
    magnitude = jnp.sqrt(square)
    sin_p = axial_speed / magnitude
    cos_p = tangent / magnitude
    blade_pitch = twist + pitch
    sin_a = sin_p * jnp.cos(blade_pitch) - cos_p * jnp.sin(blade_pitch)
    cos_a = cos_p * jnp.cos(blade_pitch) + sin_p * jnp.sin(blade_pitch)
    lift_coef = 2.0 * math.pi * sin_a * cos_a
    drag_coef = 0.02 + sin_a * sin_a
    dynamic = 0.5 * area * square
    normal = dynamic * (lift_coef * cos_p + drag_coef * sin_p)
    tangential = dynamic * (lift_coef * sin_p - drag_coef * cos_p)
    return jnp.stack([normal, -tangential * sin_t, tangential * cos_t], axis=-2)


def velocity(populations):
    lattice = jnp.asarray(LATTICE_DIRS, jnp.float32)
    density = jnp.sum(populations, axis=0)
    parts = [
        jnp.sum(populations * lattice[:, axis][:, None, None, None], axis=0) / density
        for axis in range(3)
    ]
    return jnp.stack(parts)


def collide(populations, force_field):
    lattice = jnp.asarray(LATTICE_DIRS, jnp.float32)
    weights = jnp.asarray(LATTICE_WEIGHTS, jnp.float32)[:, None, None, None]
    density = jnp.sum(populations, axis=0)
    columns = [lattice[:, axis][:, None, None, None] for axis in range(3)]
    parts = [
        (jnp.sum(populations * columns[axis], axis=0) + 0.5 * force_field[axis]) / density
        for axis in range(3)
    ]
    project = (
        columns[0] * parts[0][None] + columns[1] * parts[1][None] + columns[2] * parts[2][None]
    )
    force_proj = (
        columns[0] * force_field[0][None]
        + columns[1] * force_field[1][None]
        + columns[2] * force_field[2][None]
    )
    speed_sq = parts[0] * parts[0] + parts[1] * parts[1] + parts[2] * parts[2]
    work_rate = parts[0] * force_field[0] + parts[1] * force_field[1] + parts[2] * force_field[2]
    equilibrium = (
        weights
        * density[None]
        * (1.0 + 3.0 * project + 4.5 * project * project - 1.5 * speed_sq[None])
    )
    source = (
        (1.0 - 0.5 * OMEGA)
        * weights
        * (3.0 * (force_proj - work_rate[None]) + 9.0 * project * force_proj)
    )
    return populations - OMEGA * (populations - equilibrium) + source


def stream(padded, collided):
    x_cells = collided.shape[2]
    y_cells = collided.shape[3]
    outgoing = []
    for direction in range(19):
        shift_x = int(LATTICE_DIRS[direction, 0])
        shift_y = int(LATTICE_DIRS[direction, 1])
        shift_z = int(LATTICE_DIRS[direction, 2])
        pulled = padded[
            direction, :, 1 - shift_x : 1 - shift_x + x_cells, 1 - shift_y : 1 - shift_y + y_cells
        ]
        mirror = collided[OPPOSITE[direction]]
        if shift_z == 1:
            pulled = jnp.concatenate([mirror[:1], pulled[:-1]], axis=0)
        elif shift_z == -1:
            pulled = jnp.concatenate([pulled[1:], mirror[-1:]], axis=0)
        outgoing.append(pulled)
    return jnp.stack(outgoing)


def with_ghosts(collided):
    padded = extended(collided, (("gx", 2), ("gy", 3)), 1)
    return padded


def local(
    f_in,
    rotor_place,
    marker_cell,
    pitch_phase,
    blade_area,
    blade_twist,
    blade_speed,
    blade_angle,
    filt_in,
):
    levels = f_in.shape[1]
    x_cells = f_in.shape[2]
    y_cells = f_in.shape[3]
    rotors = rotor_place.shape[0]
    step_count = pitch_phase.shape[1]
    owned_count = filt_in.shape[2]
    spread_x = lax.axis_size("gx")
    row_slots = (rotors + spread_x - 1) // spread_x
    here_x = lax.axis_index("gx")
    here_y = lax.axis_index("gy")
    street = rotor_place[:, 0]
    plane_x = rotor_place[:, 1]
    owner_y = rotor_place[:, 2]
    rotor_ids = jnp.arange(rotors, dtype=jnp.int32)
    earlier = rotor_ids[None, :] < rotor_ids[:, None]
    same_row = street[:, None] == street[None, :]
    row_rank = jnp.sum((earlier & same_row).astype(jnp.int32), axis=1)
    same_owner = same_row & (owner_y[:, None] == owner_y[None, :])
    owner_rank = jnp.sum((earlier & same_owner).astype(jnp.int32), axis=1)
    slot_ids = jnp.arange(row_slots, dtype=jnp.int32)
    slot_pick = ((street[None, :] == here_x) & (row_rank[None, :] == slot_ids[:, None])).astype(
        jnp.int32
    )
    slot_valid = jnp.sum(slot_pick, axis=1)
    slot_rotor = jnp.sum(slot_pick * rotor_ids[None, :], axis=1)
    slot_codes = jnp.take(marker_cell, slot_rotor, axis=0)
    slot_plane = jnp.take(plane_x, slot_rotor)
    slot_pitch = pitch_angles(jnp.take(pitch_phase, slot_rotor, axis=0))
    owned_here = (jnp.take(owner_y, slot_rotor) == here_y) & (slot_valid > 0)
    owned_ids = jnp.arange(owned_count, dtype=jnp.int32)
    own_pick = (
        owned_here[None, :] & (jnp.take(owner_rank, slot_rotor)[None, :] == owned_ids[:, None])
    ).astype(jnp.float32)
    valid_float = slot_valid.astype(jnp.float32)
    start_y = here_y * y_cells
    tables = []
    for slot_index in range(row_slots):
        across, upward = stencil_tables(slot_codes[slot_index], levels, y_cells, start_y)
        tables.append((across * valid_float[slot_index], upward))
    x_ids = jnp.arange(x_cells, dtype=jnp.int32)
    filtered = filt_in[0, 0]
    own_pitch = jnp.sum(own_pick[:, :, None] * slot_pitch[None], axis=1)
    populations = f_in
    for step_index in range(step_count):
        field_speed = velocity(populations)
        samples = jnp.stack(
            [
                sample_section(
                    lax.dynamic_index_in_dim(
                        field_speed, slot_plane[slot_index], 2, keepdims=False
                    ),
                    tables[slot_index][0],
                    tables[slot_index][1],
                )
                for slot_index in range(row_slots)
            ]
        )
        sampled = lax.psum(samples, "gy")
        own_sampled = jnp.sum(own_pick[:, :, None, None] * sampled[None], axis=1)
        filtered = filtered + MIX * (own_sampled - filtered)
        own_loads = blade_loads(
            filtered,
            blade_area[0, 0],
            blade_twist[0, 0],
            blade_speed[0, 0],
            blade_angle[0, 0],
            own_pitch[:, step_index][:, None],
        )
        row_loads = jnp.sum(own_pick[:, :, None, None] * own_loads[:, None], axis=0)
        load_rows = lax.psum(row_loads, "gy")
        force_field = jnp.zeros((3, levels, x_cells, y_cells), jnp.float32)
        for slot_index in range(row_slots):
            section = spread_section(
                load_rows[slot_index], tables[slot_index][0], tables[slot_index][1]
            )
            plane_mask = (x_ids == slot_plane[slot_index]).astype(jnp.float32)
            force_field = force_field + section[:, :, None, :] * plane_mask[None, None, :, None]
        collided = collide(populations, force_field)
        populations = stream(with_ghosts(collided), collided)
    has_rotor = jnp.sum(own_pick, axis=1)[:, None, None]
    loads_out = own_loads * has_rotor
    filt_out = filtered * has_rotor
    return (populations, loads_out[None, None], filt_out[None, None])


def solution(mesh):
    in_specs = (
        P(None, None, "gx", "gy"),
        P(),
        P(),
        P(),
        P("gx", "gy", None, None),
        P("gx", "gy", None, None),
        P("gx", "gy", None, None),
        P("gx", "gy", None, None),
        P("gx", "gy", None, None, None),
    )
    out_specs = (
        P(None, None, "gx", "gy"),
        P("gx", "gy", None, None, None),
        P("gx", "gy", None, None, None),
    )
    return jax.shard_map(local, mesh=mesh, in_specs=in_specs, out_specs=out_specs, check_vma=False)
```

profile of v0, /device:TPU:1, one launch (start us, length us, event | category | flops | bytes accessed | tf_op | source)
XLA Modules:
  0.0 816.1 jit_solution(7639344466328767253)
XLA Ops:
  20.0 2.4 multiply_reduce_fusion.5
  23.2 16.3 %fusion.50 = f32[8192,3]{0,1:T(4,128)S(1)} fusion(f32[3,16,128]{2,1,0:T(8,128)S(1)} %bitcast.602, f32[]{:T(128)} %bitcast.34, f32[8192]{0:T(1024)S(1)} %get-tuple-element.179, f32[8192]{0:T(1024)S(1)} %get-tuple-element.178, f32[8192]{0:T(1024)S(1)} %get-tuple-element.177, f32[8192]{0:T(1024)S(1)} %get-tuple-element.175, s32[8192]{0:T(1024)S(1)} %get-tuple-element.170, ...), kind=kOutput, calls=%fused_computation.82 | convolution fusion | flops 618373120 | bytes 811524 | tf_op jit(solution)/shard_map/dot_general | solution.py:91
  39.6 16.2 %fusion.44 = f32[8192,3]{0,1:T(4,128)S(1)} fusion(f32[3,16,128]{2,1,0:T(8,128)S(1)} %bitcast.601, f32[]{:T(128)} %bitcast.8, f32[8192]{0:T(1024)S(1)} %get-tuple-element.157, f32[8192]{0:T(1024)S(1)} %get-tuple-element.156, f32[8192]{0:T(1024)S(1)} %get-tuple-element.155, f32[8192]{0:T(1024)S(1)} %get-tuple-element.153, s32[8192]{0:T(1024)S(1)} %get-tuple-element.148, ...), kind=kOutput, calls=%fused_computation.80 | convolution fusion | flops 618373120 | bytes 811524 | tf_op jit(solution)/shard_map/dot_general | solution.py:91
  56.0 16.4 %fusion.47 = f32[8192,3]{0,1:T(4,128)S(1)} fusion(f32[3,16,128]{2,1,0:T(8,128)S(1)} %bitcast.600, f32[]{:T(128)} %bitcast.23, f32[8192]{0:T(1024)S(1)} %get-tuple-element.168, f32[8192]{0:T(1024)S(1)} %get-tuple-element.167, f32[8192]{0:T(1024)S(1)} %get-tuple-element.166, f32[8192]{0:T(1024)S(1)} %get-tuple-element.164, s32[8192]{0:T(1024)S(1)} %get-tuple-element.159, ...), kind=kOutput, calls=%fused_computation.81 | convolution fusion | flops 618373120 | bytes 811524 | tf_op jit(solution)/shard_map/dot_general | solution.py:91
  76.9 123.7 %all-reduce.5.cloned.1.call-done = f32[3,3,8192]{2,1,0:T(4,128)} async-done(((f32[3,3,8192]{2,1,0:T(4,128)}), f32[3,3,8192]{2,1,0:T(4,128)}) %all-reduce.5.cloned.1.call-update) | async-done | bytes 294928 | tf_op jit(solution)/shard_map/psum | solution.py:273
  200.6 1.5 multiply_reduce_fusion.9
  202.2 1.4 add_multiply_fusion.17
  205.1 1.6 multiply_reduce_fusion.8
  208.8 122.4 %all-reduce.7.cloned.1.call-done = f32[3,3,8192]{2,1,0:T(4,128)} async-done(((f32[3,3,8192]{2,1,0:T(4,128)}), f32[3,3,8192]{2,1,0:T(4,128)}) %all-reduce.7.cloned.1.call-update) | async-done | bytes 294928 | tf_op jit(solution)/shard_map/psum | solution.py:285
  332.4 8.6 %fusion.62 = f32[3,16,128]{2,1,0:T(8,128)S(1)} fusion(f32[]{:T(128)} %bitcast.8, f32[8192]{0:T(1024)} %copy-done.68, f32[8192]{0:T(1024)} %copy-done.66, f32[8192]{0:T(1024)} %copy-done.64, f32[8192]{0:T(1024)S(1)} %copy-done.48, s32[8192]{0:T(1024)S(1)} %get-tuple-element.148, s32[128]{0:T(128)S(1)} %copy-done.120, f32[8192,3]{0,1:T(4,128)S(1)} %get-tuple-element.131, ...), kind=kOutput, calls=%fused_computation.86 | convolution fusion | flops 618010624 | bytes 811524 | tf_op jit(solution)/shard_map/dot_general | solution.py:104
  341.1 7.9 fusion.82
  349.1 8.3 %fusion.72 = f32[3,16,128]{2,1,0:T(8,128)S(1)} fusion(f32[]{:T(128)} %bitcast.23, f32[8192]{0:T(1024)S(1)} %copy-done.77, f32[8192]{0:T(1024)S(1)} %copy-done.74, f32[8192]{0:T(1024)S(1)} %copy-done.71, f32[8192]{0:T(1024)S(1)} %copy-done.54, s32[8192]{0:T(1024)S(1)} %copy-done.51, s32[128]{0:T(128)S(1)} %copy-done.120, ...), kind=kOutput, calls=%fused_computation.88 | convolution fusion | flops 618010624 | bytes 811524 | tf_op jit(solution)/shard_map/dot_general | solution.py:104
  359.1 2.5 fusion.24
  362.5 5.2 collective-permute-start.1
  368.3 2.0 collective-permute-done.1
  370.4 5.5 collective-permute-done
  376.5 4.4 fusion.415
  380.9 4.1 copy.171
  385.0 4.1 copy.169
  389.1 1.8 collective-permute-start.3
  394.0 5.9 copy.172
  399.9 5.6 copy.170
  405.5 1.9 constant_dynamic-update-slice_fusion.5
  410.0 1.4 copy-done.8
  414.6 16.4 %fusion.59 = f32[8192,3]{0,1:T(4,128)S(1)} fusion(f32[3,16,128]{2,1,0:T(8,128)S(1)} %bitcast.605, f32[]{:T(128)} %bitcast.34, f32[8192]{0:T(1024)S(1)} %copy-done.89, f32[8192]{0:T(1024)S(1)} %copy-done.85, f32[8192]{0:T(1024)S(1)} %copy-done.81, f32[8192]{0:T(1024)S(1)} %copy-done.62, s32[8192]{0:T(1024)S(1)} %copy-done.58, s32[128]{0:T(128)S(1)} %copy-done.121, ...), kind=kOutput, calls=%fused_computation.85 | convolution fusion | flops 618373120 | bytes 811524 | tf_op jit(solution)/shard_map/dot_general | solution.py:91
  431.1 16.4 %fusion.56 = f32[8192,3]{0,1:T(4,128)S(1)} fusion(f32[3,16,128]{2,1,0:T(8,128)S(1)} %bitcast.604, f32[]{:T(128)} %bitcast.23, f32[8192]{0:T(1024)S(1)} %copy-done.78, f32[8192]{0:T(1024)S(1)} %copy-done.75, f32[8192]{0:T(1024)S(1)} %copy-done.72, f32[8192]{0:T(1024)S(1)} %copy-done.55, s32[8192]{0:T(1024)S(1)} %copy-done.52, s32[128]{0:T(128)S(1)} %copy-done.121, ...), kind=kOutput, calls=%fused_computation.84 | convolution fusion | flops 618373120 | bytes 811524 | tf_op jit(solution)/shard_map/dot_general | solution.py:91
  447.6 16.3 %fusion.53 = f32[8192,3]{0,1:T(4,128)S(1)} fusion(f32[3,16,128]{2,1,0:T(8,128)S(1)} %bitcast.603, f32[]{:T(128)} %bitcast.8, f32[8192]{0:T(1024)S(1)} %copy-done.69, f32[8192]{0:T(1024)S(1)} %copy-done.67, f32[8192]{0:T(1024)S(1)} %copy-done.65, f32[8192]{0:T(1024)S(1)} %copy-done.49, s32[8192]{0:T(1024)S(1)} %copy-done.46, s32[128]{0:T(128)S(1)} %copy-done.121, ...), kind=kOutput, calls=%fused_computation.83 | convolution fusion | flops 618373120 | bytes 811524 | tf_op jit(solution)/shard_map/dot_general | solution.py:91
  465.0 124.3 %all-reduce.9.cloned.1.call-done = f32[3,3,8192]{2,1,0:T(4,128)} async-done(((f32[3,3,8192]{2,1,0:T(4,128)}), f32[3,3,8192]{2,1,0:T(4,128)}) %all-reduce.9.cloned.1.call-update) | async-done | bytes 294928 | tf_op jit(solution)/shard_map/psum | solution.py:273
  589.3 1.5 multiply_reduce_fusion.7
  590.9 1.6 add_multiply_fusion.15
  594.0 1.6 multiply_reduce_fusion.6
  596.7 123.5 %all-reduce.11.cloned.1.call-done = f32[3,3,8192]{2,1,0:T(4,128)} async-done(((f32[3,3,8192]{2,1,0:T(4,128)}), f32[3,3,8192]{2,1,0:T(4,128)}) %all-reduce.11.cloned.1.call-update) | async-done | bytes 294928 | tf_op jit(solution)/shard_map/psum | solution.py:285
  721.4 8.7 %fusion.77 = f32[3,16,128]{2,1,0:T(8,128)S(1)} fusion(f32[]{:T(128)} %bitcast.23, f32[8192]{0:T(1024)} %copy-done.76, f32[8192]{0:T(1024)} %copy-done.73, f32[8192]{0:T(1024)} %copy-done.70, f32[8192]{0:T(1024)S(1)} %copy-done.55, s32[8192]{0:T(1024)S(1)} %copy-done.52, s32[128]{0:T(128)} %copy-done.119, f32[8192,3]{0,1:T(4,128)S(1)} %get-tuple-element.123, ...), kind=kOutput, calls=%fused_computation.89 | convolution fusion | flops 618010624 | bytes 811524 | tf_op jit(solution)/shard_map/dot_general | solution.py:104
  730.1 7.8 fusion.87
  738.0 8.1 fusion.67
  747.9 2.5 fusion.31
  751.5 5.2 collective-permute-start.5
  756.6 2.7 collective-permute-done.5
  759.3 5.5 collective-permute-done.4
  765.5 4.4 fusion.414
  769.9 4.1 copy.175
  774.0 3.5 copy.173
  777.8 1.9 collective-permute-start.7
  781.2 1.6 collective-permute-done.7
  782.8 5.6 copy.176
  788.4 5.7 copy.174
  794.1 1.9 maximum_dynamic-update-slice_fusion.5
  801.0 1.9 maximum_dynamic-update-slice_fusion.1
  (377 shorter events, 50.6 us)
Async XLA Ops:
  7.2 193.3 %all-reduce.5.cloned.1.call-start = ((), (), s32[]{:S(2)}) async-start(), calls=%async_computation | async-start | bytes 786432 | tf_op jit(solution)/shard_map/psum | solution.py:273
  16.1 39.8 %copy-start.50 = (s32[8192]{0:T(1024)}, s32[8192]{0:T(1024)S(1)}, u32[]{:S(2)}) copy-start(s32[8192]{0:T(1024)S(1)} %get-tuple-element.159) | copy-start | bytes 98308
  16.3 39.6 %copy-start.53 = (f32[8192]{0:T(1024)}, f32[8192]{0:T(1024)S(1)}, u32[]{:S(2)}) copy-start(f32[8192]{0:T(1024)S(1)} %get-tuple-element.164) | copy-start | bytes 98308
  16.4 316.0 %copy-start.45 = (s32[8192]{0:T(1024)}, s32[8192]{0:T(1024)S(1)}, u32[]{:S(2)}) copy-start(s32[8192]{0:T(1024)S(1)} %get-tuple-element.148) | copy-start | bytes 98308
  16.6 23.0 %copy-start.47 = (f32[8192]{0:T(1024)}, f32[8192]{0:T(1024)S(1)}, u32[]{:S(2)}) copy-start(f32[8192]{0:T(1024)S(1)} %get-tuple-element.153) | copy-start | bytes 98308
  17.0 22.6 %copy-start.60 = (f32[8192]{0:T(1024)}, f32[8192]{0:T(1024)S(1)}, u32[]{:S(2)}) copy-start(f32[8192]{0:T(1024)S(1)} %get-tuple-element.175) | copy-start | bytes 98308
  17.0 38.9 %copy-start.119 = (s32[128]{0:T(128)}, s32[128]{0:T(128)S(1)}, u32[]{:S(2)}) copy-start(s32[128]{0:T(128)S(1)} %iota_add_fusion) | copy-start | bytes 1540
  17.7 38.2 %copy-start.70 = (f32[8192]{0:T(1024)}, f32[8192]{0:T(1024)S(1)}, u32[]{:S(2)}) copy-start(f32[8192]{0:T(1024)S(1)} %get-tuple-element.166) | copy-start | bytes 98308
  17.7 38.2 %copy-start.73 = (f32[8192]{0:T(1024)}, f32[8192]{0:T(1024)S(1)}, u32[]{:S(2)}) copy-start(f32[8192]{0:T(1024)S(1)} %get-tuple-element.167) | copy-start | bytes 98308
  17.7 38.2 %copy-start.76 = (f32[8192]{0:T(1024)}, f32[8192]{0:T(1024)S(1)}, u32[]{:S(2)}) copy-start(f32[8192]{0:T(1024)S(1)} %get-tuple-element.168) | copy-start | bytes 98308
  17.9 21.7 %copy-start.64 = (f32[8192]{0:T(1024)}, f32[8192]{0:T(1024)S(1)}, u32[]{:S(2)}) copy-start(f32[8192]{0:T(1024)S(1)} %get-tuple-element.155) | copy-start | bytes 98308
  17.9 21.7 %copy-start.66 = (f32[8192]{0:T(1024)}, f32[8192]{0:T(1024)S(1)}, u32[]{:S(2)}) copy-start(f32[8192]{0:T(1024)S(1)} %get-tuple-element.156) | copy-start | bytes 98308
  17.9 21.7 %copy-start.68 = (f32[8192]{0:T(1024)}, f32[8192]{0:T(1024)S(1)}, u32[]{:S(2)}) copy-start(f32[8192]{0:T(1024)S(1)} %get-tuple-element.157) | copy-start | bytes 98308
  18.0 21.6 %copy-start.79 = (f32[8192]{0:T(1024)}, f32[8192]{0:T(1024)S(1)}, u32[]{:S(2)}) copy-start(f32[8192]{0:T(1024)S(1)} %get-tuple-element.177) | copy-start | bytes 98308
  18.0 21.6 %copy-start.83 = (f32[8192]{0:T(1024)}, f32[8192]{0:T(1024)S(1)}, u32[]{:S(2)}) copy-start(f32[8192]{0:T(1024)S(1)} %get-tuple-element.178) | copy-start | bytes 98308
  18.0 21.6 %copy-start.87 = (f32[8192]{0:T(1024)}, f32[8192]{0:T(1024)S(1)}, u32[]{:S(2)}) copy-start(f32[8192]{0:T(1024)S(1)} %get-tuple-element.179) | copy-start | bytes 98308
  22.7 318.3 %copy-start.28 = (f32[8192,16]{0,1:T(8,128)}, f32[8192,16]{0,1:T(8,128)S(1)}, u32[]{:S(2)}) copy-start(f32[8192,16]{0,1:T(8,128)S(1)} %select_add_fusion) | copy-start | bytes 1572868
  23.0 309.4 %copy-start.26 = (f32[8192,16]{0,1:T(8,128)}, f32[8192,16]{0,1:T(8,128)S(1)}, u32[]{:S(2)}) copy-start(f32[8192,16]{0,1:T(8,128)S(1)} %select_add_fusion.2) | copy-start | bytes 1572868
  23.2 325.8 %copy-start.31 = (f32[8192,16]{0,1:T(8,128)}, f32[8192,16]{0,1:T(8,128)S(1)}, u32[]{:S(2)}) copy-start(f32[8192,16]{0,1:T(8,128)S(1)} %select_add_fusion.1) | copy-start | bytes 1572868
  56.0 146.0 %copy-start.22 = (f32[1,1,2,3,8192]{4,2,3,1,0:T(2,128)S(1)}, f32[1,1,2,3,8192]{4,2,3,1,0:T(2,128)}, u32[]{:S(2)}) copy-start(f32[1,1,2,3,8192]{4,2,3,1,0:T(2,128)} %param.25) | copy-start | bytes 589828
  56.0 146.2 %copy-start.19 = (f32[1,1,2,8192]{3,2,1,0:T(2,128)S(1)}, f32[1,1,2,8192]{3,2,1,0:T(2,128)}, u32[]{:S(2)}) copy-start(f32[1,1,2,8192]{3,2,1,0:T(2,128)} %param.22) | copy-start | bytes 196612
  56.0 146.2 %copy-start.20 = (f32[1,1,2,8192]{3,2,1,0:T(2,128)S(1)}, f32[1,1,2,8192]{3,2,1,0:T(2,128)}, u32[]{:S(2)}) copy-start(f32[1,1,2,8192]{3,2,1,0:T(2,128)} %param.21) | copy-start | bytes 196612
  56.0 146.2 %copy-start.33 = (f32[1,1,2,8192]{3,2,1,0:T(2,128)S(1)}, f32[1,1,2,8192]{3,2,1,0:T(2,128)}, u32[]{:S(2)}) copy-start(f32[1,1,2,8192]{3,2,1,0:T(2,128)} %param.23) | copy-start | bytes 196612
  72.4 259.9 %copy-start.48 = (f32[8192]{0:T(1024)S(1)}, f32[8192]{0:T(1024)}, u32[]{:S(2)}) copy-start(f32[8192]{0:T(1024)} %copy-done.47) | copy-start | bytes 98308
  73.3 259.1 %copy-start.120 = (s32[128]{0:T(128)S(1)}, s32[128]{0:T(128)}, u32[]{:S(2)}) copy-start(s32[128]{0:T(128)} %copy-done.119) | copy-start | bytes 1540
  73.3 257.9 %all-reduce.7.cloned.1.call-start = ((), (), s32[]{:S(2)}) async-start(), calls=%async_computation.1 | async-start | bytes 786432 | tf_op jit(solution)/shard_map/psum | solution.py:285
  75.9 265.1 %copy-start.43 = (f32[2,3]{0,1:T(4,128)}, f32[2,3]{0,1:T(4,128)S(1)}, u32[]{:S(2)}) copy-start(f32[2,3]{0,1:T(4,128)S(1)} %copy.166) | copy-start | bytes 76
  206.7 382.6 %all-reduce.9.cloned.1.call-start = ((), (), s32[]{:S(2)}) async-start(), calls=%async_computation.2 | async-start | bytes 786432 | tf_op jit(solution)/shard_map/psum | solution.py:273
  207.6 149.8 %copy-start.112 = (f32[16]{0:T(128)}, f32[16]{0:T(128)S(1)}, u32[]{:S(2)}) copy-start(f32[16]{0:T(128)S(1)} %compare_convert_fusion.2) | copy-start | bytes 196
  208.3 149.2 %copy-start.114 = (f32[16]{0:T(128)}, f32[16]{0:T(128)S(1)}, u32[]{:S(2)}) copy-start(f32[16]{0:T(128)S(1)} %compare_convert_fusion) | copy-start | bytes 196
  208.8 148.6 %copy-start.116 = (f32[16]{0:T(128)}, f32[16]{0:T(128)S(1)}, u32[]{:S(2)}) copy-start(f32[16]{0:T(128)S(1)} %compare_convert_fusion.1) | copy-start | bytes 196
  362.5 7.8 collective-permute-start.1
  367.7 8.2 %collective-permute-start = (f32[19,16,1,128]{3,2,1,0:T(1,128)S(1)}, f32[19,16,1,128]{3,2,1,0:T(1,128)S(1)}, u32[]{:S(2)}, u32[]{:S(2)}) collective-permute-start(f32[19,16,1,128]{3,2,1,0:T(1,128)S(1)} %get-tuple-element.116), channel_id=1, source_target_pairs={{0,16},{16,32},{32,48},{48,64},{64,80},{80,96},{96,112},{112,128},... | collective-permute-start | bytes 466952 | tf_op jit(solution)/shard_map/ppermute | solution.py:49
  368.3 44.5 %copy-start.35 = (f32[1,16,128]{2,1,0:T(8,128)}, f32[1,16,128]{2,1,0:T(8,128)S(1)}, u32[]{:S(2)}) copy-start(f32[1,16,128]{2,1,0:T(8,128)S(1)} %get-tuple-element.106) | copy-start | bytes 24580
  389.1 10.8 %collective-permute-start.2 = (f32[19,16,18,1]{0,1,3,2:T(8,128)}, f32[19,16,18,1]{0,1,3,2:T(8,128)}, u32[]{:S(2)}, u32[]{:S(2)}) collective-permute-start(f32[19,16,18,1]{0,1,3,2:T(8,128)} %copy.169), channel_id=1, source_target_pairs={{0,1},{1,2},{2,3},{3,4},{4,5},{5,6},{6,7},{7,8},{8,9},{9,10},{10,1... | collective-permute-start | bytes 65672 | tf_op jit(solution)/shard_map/ppermute | solution.py:49
  389.1 4.9 collective-permute-start.3
  391.7 21.1 %copy-start.14 = (f32[15,16,128]{2,1,0:T(8,128)}, f32[15,16,128]{2,1,0:T(8,128)S(1)}, u32[]{:S(2)}) copy-start(f32[15,16,128]{2,1,0:T(8,128)S(1)} %get-tuple-element.85) | copy-start | bytes 368644
  447.6 141.7 %copy-start.44 = (f32[2,3]{0,1:T(4,128)S(1)}, f32[2,3]{0,1:T(4,128)}, u32[]{:S(2)}) copy-start(f32[2,3]{0,1:T(4,128)} %copy-done.43) | copy-start | bytes 76
  447.6 143.3 %copy-start.21 = (f32[1,1,2,8192]{3,2,1,0:T(2,128)S(1)}, f32[1,1,2,8192]{3,2,1,0:T(2,128)}, u32[]{:S(2)}) copy-start(f32[1,1,2,8192]{3,2,1,0:T(2,128)} %param.21) | copy-start | bytes 196612
  447.6 143.3 %copy-start.34 = (f32[1,1,2,8192]{3,2,1,0:T(2,128)S(1)}, f32[1,1,2,8192]{3,2,1,0:T(2,128)}, u32[]{:S(2)}) copy-start(f32[1,1,2,8192]{3,2,1,0:T(2,128)} %param.23) | copy-start | bytes 196612
  447.6 143.3 %copy-start.103 = (f32[2]{0:T(128)S(1)}, f32[2]{0:T(128)}, u32[]{:S(2)}) copy-start(f32[2]{0:T(128)} %get-tuple-element.17) | copy-start | bytes 28
  463.9 131.7 %copy-start.23 = (f32[1,1,2,3,8192]{4,2,3,1,0:T(2,128)S(1)}, f32[1,1,2,3,8192]{4,2,3,1,0:T(2,128)}, u32[]{:S(2)}) copy-start(f32[1,1,2,3,8192]{4,2,3,1,0:T(2,128)} %param.25) | copy-start | bytes 589828
  464.8 255.4 %all-reduce.11.cloned.1.call-start = ((), (), s32[]{:S(2)}) async-start(), calls=%async_computation.3 | async-start | bytes 786432 | tf_op jit(solution)/shard_map/psum | solution.py:285
  750.4 49.8 %copy-start.2 = (f32[19,16,16,128]{3,2,1,0:T(8,128)}, f32[19,16,16,128]{3,2,1,0:T(8,128)S(1)}, u32[]{:S(2)}) copy-start(f32[19,16,16,128]{3,2,1,0:T(8,128)S(1)} %fusion.31) | copy-start | bytes 7471108
  751.5 7.8 collective-permute-start.5
  756.6 8.2 %collective-permute-start.4 = (f32[19,16,1,128]{3,2,1,0:T(1,128)S(1)}, f32[19,16,1,128]{3,2,1,0:T(1,128)S(1)}, u32[]{:S(2)}, u32[]{:S(2)}) collective-permute-start(f32[19,16,1,128]{3,2,1,0:T(1,128)S(1)} %get-tuple-element.101), channel_id=1, source_target_pairs={{0,16},{16,32},{32,48},{48,64},{64,80},{80,96},{96,112},{112,128},... | collective-permute-start | bytes 466952 | tf_op jit(solution)/shard_map/ppermute | solution.py:49
  777.4 11.0 %collective-permute-start.6 = (f32[19,16,18,1]{0,1,3,2:T(8,128)S(1)}, f32[19,16,18,1]{0,1,3,2:T(8,128)}, u32[]{:S(2)}, u32[]{:S(2)}) collective-permute-start(f32[19,16,18,1]{0,1,3,2:T(8,128)S(1)} %copy.173), channel_id=1, source_target_pairs={{0,1},{1,2},{2,3},{3,4},{4,5},{5,6},{6,7},{7,8},{8,9},{9,10},{10,1... | collective-permute-start | bytes 65672 | tf_op jit(solution)/shard_map/ppermute | solution.py:49
  777.8 5.0 collective-permute-start.7
  (87 other events, 692.4 us)
Sparse Core Ops, SparseCore 0:
  73.4 127.0 all-reduce.4
  206.8 124.3 all-reduce.6
  464.9 124.3 all-reduce.8
  595.7 124.3 all-reduce.10
where the time goes:
time: 827 us; the launch traced here: 816 us
  waiting for transfers between devices  512 us (62%)
  matrix products  147 us (18%)
  local copies, waits for them, and re-layouts  67 us (8%)
  other arithmetic  52.7 us (6%)
  between operations  22.1 us (3%)
  starting transfers between devices  14.8 us (2%)
    psum x2, waiting for transfers between devices, local(): sampled = lax.psum(samples, 'gy')  248 us
    psum x2, waiting for transfers between devices, local(): load_rows = lax.psum(row_loads, 'gy')  246 us
    dot_general x6, matrix products, sample_section(): jnp.dot(across, flattened, precision=lax.Precision.HIGHEST, preferred_ele...  98 us
    dot_general x6, matrix products, spread_section(): lax.dot_general(weighted, across, (((0,), (0,)), ((), ())), precision=lax...  49.3 us
    unnamed x34, other arithmetic  19.7 us
    slice x6, local copies, waits for them, and re-layouts, extended(): lax.slice_in_dim(block, 0, width, axis=dim)  17.4 us
  transfers between devices with their start and end apart: 12, of which 10 were waited for; matrix products, arithmetic and copies ran while one was open for 3% of the time, Pallas kernels for 0%

commit v1 on v0

v1 whole, which is shorter than its diff:
```python
import functools
import math

import jax
import jax.numpy as jnp
import numpy as np
from jax import lax
from jax.experimental import pallas as pl
from jax.experimental.pallas import tpu as pltpu
from jax.sharding import PartitionSpec as P

DIRS = [
    (0, 0, 0),
    (1, 0, 0), (-1, 0, 0), (0, 1, 0), (0, -1, 0), (0, 0, 1), (0, 0, -1),
    (1, 1, 0), (-1, -1, 0), (1, -1, 0), (-1, 1, 0),
    (1, 0, 1), (-1, 0, -1), (1, 0, -1), (-1, 0, 1),
    (0, 1, 1), (0, -1, -1), (0, 1, -1), (0, -1, 1),
]
OPPOSITE = [0, 2, 1, 4, 3, 6, 5, 8, 7, 10, 9, 12, 11, 14, 13, 16, 15, 18, 17]
WEIGHTS = [1.0 / 3.0] + [1.0 / 18.0] * 6 + [1.0 / 36.0] * 12
PAIRS = [(1, 2), (3, 4), (5, 6), (7, 8), (9, 10), (11, 12), (13, 14), (15, 16), (17, 18)]
OMEGA = 1.0 / 0.6
SPREAD = 0.01
MIX = 0.5
PITCH_AMP = 0.2
PHASES = 64

NQ = 19
LEVELS = 16
CX = 16
CY = 128
SLOTS = 3
ROWS = SLOTS * 2 * 3 * LEVELS
REDUCERS = 12
SHARD = ROWS // REDUCERS
TILES = 16
F32 = jnp.float32
MESH = pl.DeviceIdType.MESH

X_PLUS = [q for q in range(NQ) if DIRS[q][0] == 1]
X_MINUS = [q for q in range(NQ) if DIRS[q][0] == -1]
Y_PLUS = [q for q in range(NQ) if DIRS[q][1] == 1]
Y_MINUS = [q for q in range(NQ) if DIRS[q][1] == -1]


def peskin(offsets):
    distance = jnp.abs(offsets)
    near_arg = jnp.maximum(1.0 + 4.0 * distance - 4.0 * distance * distance, 1.0)
    far_arg = jnp.maximum(-7.0 + 12.0 * distance - 4.0 * distance * distance, 1.0)
    near_part = (3.0 - 2.0 * distance + jnp.sqrt(near_arg)) / 8.0
    far_part = (5.0 - 2.0 * distance - jnp.sqrt(far_arg)) / 8.0
    return jnp.where(distance <= 1.0, near_part, far_part)


def signed_sum(terms):
    total = None
    for sign, value in terms:
        if total is None:
            total = value if sign > 0 else -value
        else:
            total = total + value if sign > 0 else total - value
    return total


def moments(pops):
    density = pops[0]
    for q in range(1, NQ):
        density = density + pops[q]
    momentum = [
        signed_sum([(DIRS[q][axis], pops[q]) for q in range(NQ) if DIRS[q][axis] != 0])
        for axis in range(3)
    ]
    return density, momentum


def along(direction, vector):
    return signed_sum([(direction[axis], vector[axis]) for axis in range(3) if direction[axis]])


def collide(pops, force):
    density, momentum = moments(pops)
    inverse = 1.0 / density
    if force is not None:
        momentum = [momentum[axis] + 0.5 * force[axis] for axis in range(3)]
    vel = [momentum[axis] * inverse for axis in range(3)]
    speed_sq = vel[0] * vel[0] + vel[1] * vel[1] + vel[2] * vel[2]
    keep = 1.0 - OMEGA
    scaled = OMEGA * density
    base = scaled * (1.0 - 1.5 * speed_sq)
    if force is not None:
        half = 1.0 - 0.5 * OMEGA
        work = vel[0] * force[0] + vel[1] * force[1] + vel[2] * force[2]
        base = base - (3.0 * half) * work
    out = [None] * NQ
    out[0] = keep * pops[0] + WEIGHTS[0] * base
    for first, second in PAIRS:
        project = along(DIRS[first], vel)
        even = base + scaled * (4.5 * project * project)
        odd = scaled * (3.0 * project)
        if force is not None:
            pull = along(DIRS[first], force)
            even = even + (9.0 * half) * (project * pull)
            odd = odd + (3.0 * half) * pull
        weight = WEIGHTS[first]
        out[first] = keep * pops[first] + weight * (even + odd)
        out[second] = keep * pops[second] + weight * (even - odd)
    return out


def split(value):
    high = value.astype(jnp.bfloat16)
    low = (value - high.astype(F32)).astype(jnp.bfloat16)
    return high, low


def mega(
    f_ref, rp_ref, mc_ref, pp_ref, area_ref, twist_ref, speed_ref, angle_ref, filt_ref,
    fo_ref, lo_ref, io_ref,
    post, fnext, plane_f, plane_p, win_tx, rs_rx, win_rx, bl_tx, bl_rx, ou_tx, ou_rx,
    w_hi, w_lo, up_ref, val_ref,
    xs_tx, xs_rx, ys_tx, ys_rx, cr_rx,
    rs_s, rs_r, ag_s, ag_r, bl_s, bl_r, ou_s, ou_r, ha_s, ha_r,
):
    me_x = lax.axis_index("gx")
    me = lax.axis_index("gy")
    count_x = lax.axis_size("gx")
    steps = pp_ref.shape[1]
    rotors = rp_ref.shape[0]
    chunk = bl_tx.shape[3]
    x_up = lax.rem(me_x + 1, count_x)
    x_dn = lax.rem(me_x + count_x - 1, count_x)
    y_up = lax.rem(me + 1, TILES)
    y_dn = lax.rem(me + TILES - 1, TILES)

    barrier = pltpu.get_barrier_semaphore()

    def greet(k, carry):
        pl.semaphore_signal(
            barrier, inc=1, device_id={"gy": lax.rem(me + k, TILES)}, device_id_type=MESH
        )
        return carry

    lax.fori_loop(1, TILES, greet, 0)
    for other_x in (x_up, x_dn):
        pl.semaphore_signal(barrier, inc=1, device_id={"gx": other_x}, device_id_type=MESH)
        for other_y in (y_up, y_dn):
            pl.semaphore_signal(
                barrier, inc=1, device_id={"gx": other_x, "gy": other_y}, device_id_type=MESH
            )

    def exchange_start(src, dst, send, recv):
        def body(k, carry):
            to = lax.rem(me + k, TILES)
            pltpu.make_async_remote_copy(
                src_ref=src(to), dst_ref=dst, send_sem=send.at[k], recv_sem=recv.at[k],
                device_id={"gy": to}, device_id_type=MESH,
            ).start()
            return carry

        lax.fori_loop(1, TILES, body, 0)

    def exchange_wait(ref, sems, which):
        def body(k, carry):
            handle = pltpu.make_async_remote_copy(
                src_ref=ref, dst_ref=ref, send_sem=sems.at[k], recv_sem=sems.at[k],
                device_id={"gy": lax.rem(me + k, TILES)}, device_id_type=MESH,
            )
            if which == "recv":
                handle.wait_recv()
            else:
                handle.wait_send()
            return carry

        lax.fori_loop(1, TILES, body, 0)

    def reducer_of(tile):
        return lax.rem(tile, 4) < 3, (tile // 4) * 3 + lax.rem(tile, 4)

    is_reducer, my_shard = reducer_of(me)

    def scatter_start(turn):
        def body(k, carry):
            to = lax.rem(me + k, TILES)
            active, shard = reducer_of(to)

            @pl.when(active)
            def _():
                pltpu.make_async_remote_copy(
                    src_ref=win_tx.at[turn, shard], dst_ref=rs_rx.at[turn, me],
                    send_sem=rs_s.at[turn, k], recv_sem=rs_r.at[turn, k],
                    device_id={"gy": to}, device_id_type=MESH,
                ).start()

            return carry

        lax.fori_loop(1, TILES, body, 0)

    def scatter_finish(turn):
        @pl.when(is_reducer)
        def _():
            exchange_wait(rs_rx.at[turn, 0], rs_r.at[turn], "recv")
            rs_rx[turn, me] = win_tx[turn, my_shard]
            total = rs_rx[turn, 0]
            for source in range(1, TILES):
                total = total + rs_rx[turn, source]
            win_rx[turn, my_shard] = total
            exchange_start(
                lambda to: win_rx.at[turn, my_shard], win_rx.at[turn, my_shard],
                ag_s.at[turn], ag_r.at[turn],
            )

    def gather_wait(turn):
        def body(k, carry):
            source = lax.rem(me - k + TILES, TILES)
            active, shard = reducer_of(source)

            @pl.when(active)
            def _():
                pltpu.make_async_remote_copy(
                    src_ref=win_rx.at[turn, 0], dst_ref=win_rx.at[turn, 0],
                    send_sem=ag_s.at[turn, k], recv_sem=ag_r.at[turn, k],
                    device_id={"gy": source}, device_id_type=MESH,
                ).wait_recv()

            return carry

        lax.fori_loop(1, TILES, body, 0)

    def sends_done(turn):
        def body(k, carry):
            active, shard = reducer_of(lax.rem(me + k, TILES))

            @pl.when(active)
            def _():
                pltpu.make_async_remote_copy(
                    src_ref=win_tx.at[turn, 0], dst_ref=win_tx.at[turn, 0],
                    send_sem=rs_s.at[turn, k], recv_sem=rs_r.at[turn, k],
                    device_id={"gy": lax.rem(me + k, TILES)}, device_id_type=MESH,
                ).wait_send()

            return carry

        lax.fori_loop(1, TILES, body, 0)

        @pl.when(is_reducer)
        def _():
            exchange_wait(win_rx.at[turn, 0], ag_s.at[turn], "send")

    def find(r, carry):
        count, ids, planes, owners = carry
        here = (rp_ref[r, 0] == me_x).astype(jnp.int32)
        new_ids, new_planes, new_owners = [], [], []
        for s in range(SLOTS):
            take = here * (count == s).astype(jnp.int32)
            new_ids.append(ids[s] + take * r)
            new_planes.append(planes[s] + take * rp_ref[r, 1])
            new_owners.append(owners[s] + take * rp_ref[r, 2])
        return count + here, tuple(new_ids), tuple(new_planes), tuple(new_owners)

    zero = jnp.int32(0)
    count, ids, planes, owners = lax.fori_loop(
        0, rotors, find, (zero, (zero,) * SLOTS, (zero,) * SLOTS, (zero,) * SLOTS)
    )
    valid = [(count > s).astype(jnp.int32) for s in range(SLOTS)]
    ranks = [
        jnp.minimum(sum([(owners[s] == owners[e]).astype(jnp.int32) for e in range(s)], zero), 1)
        for s in range(SLOTS)
    ]

    firsts = []
    for s in range(SLOTS):
        codes = mc_ref[pl.ds(ids[s], 1), :]
        lowest = jnp.min(codes, axis=1, keepdims=True)
        firsts.append(jnp.minimum(lowest // (64 * LEVELS * CY), TILES - 2))

    level_shape = (LEVELS, CY)

    def sections(source, turn):
        for s in range(SLOTS):
            pops = [source[q, :, planes[s], :] for q in range(NQ)]
            for q in range(NQ):
                plane_f[s, q] = pops[q]
            density, momentum = moments(pops)
            inverse = 1.0 / density
            first = jnp.broadcast_to(firsts[s], level_shape)
            for half in range(2):
                inside = first == me - half
                for axis in range(3):
                    row = s * 96 + half * 48 + axis * LEVELS
                    value = jnp.where(inside, momentum[axis] * inverse, 0.0)
                    for part in range(2):
                        at = row + 8 * part
                        win_tx[turn, at // SHARD, at % SHARD : at % SHARD + 8, :] = value[
                            8 * part : 8 * part + 8
                        ]

    def window(turn, s, half):
        parts = []
        for block in range(6):
            at = s * 96 + half * 48 + 8 * block
            parts.append(win_rx[turn, at // SHARD, at % SHARD : at % SHARD + 8, :])
        return jnp.concatenate(parts, axis=0)

    def collide_levels(source, low, high):
        def body(z, carry):
            out = collide([source[q, z] for q in range(NQ)], None)
            for q in range(NQ):
                post[q, z] = out[q]
            return carry

        lax.fori_loop(low, high, body, 0)

    sections(f_ref, 0)
    pl.semaphore_wait(barrier, TILES - 1 + 6)
    scatter_start(0)

    def fill(d, carry):
        lanes = pl.ds(pl.multiple_of(d * chunk, chunk), chunk)
        for e in range(2):
            for k, ref in enumerate((area_ref, twist_ref, speed_ref, angle_ref)):
                bl_tx[d, e, k : k + 1, :] = ref[e : e + 1, lanes]
            for axis in range(3):
                bl_tx[d, e, 4 + axis : 5 + axis, :] = filt_ref[e, axis : axis + 1, lanes]
            bl_tx[d, e, 7:8, :] = jnp.zeros((1, chunk), F32)
        return carry

    lax.fori_loop(0, TILES, fill, 0)
    exchange_start(lambda to: bl_tx.at[to], bl_rx.at[me], bl_s, bl_r)

    lanes = pl.ds(pl.multiple_of(me * chunk, chunk), chunk)
    for s in range(SLOTS):
        codes = mc_ref[pl.ds(ids[s], 1), lanes]
        fraction_z = (codes % 8).astype(F32) / 8.0
        fraction_y = (codes // 8 % 8).astype(F32) / 8.0
        cell_z = codes // 64 % LEVELS
        cell_y = codes // (64 * LEVELS)
        weights_y = [peskin(corner - 1.0 - fraction_y) for corner in range(4)]
        weights_z = [peskin(corner - 1.0 - fraction_z) for corner in range(4)]
        gap = lax.broadcasted_iota(jnp.int32, (LEVELS, chunk), 0) - cell_z
        upward = jnp.zeros((LEVELS, chunk), F32)
        for corner in range(4):
            upward = jnp.where(gap == corner, weights_z[corner], upward)
        up_ref[s] = upward
        anchor = cell_y - firsts[s] * CY
        for part in range(8):
            gap = lax.broadcasted_iota(jnp.int32, (32, chunk), 0) + 32 * part - anchor
            across = jnp.zeros((32, chunk), F32)
            for corner in range(4):
                across = jnp.where(gap == corner, weights_y[corner], across)
            high, low = split(across)
            w_hi[s, 32 * part : 32 * part + 32, :] = high
            w_lo[s, 32 * part : 32 * part + 32, :] = low

    blade = {}
    x_ids = lax.broadcasted_iota(jnp.int32, (CX, CY), 0)
    y_ids = lax.broadcasted_iota(jnp.int32, (CX, CY), 1)
    last_filtered = None

    for step in range(steps):
        source = f_ref if step == 0 else fnext
        target = fo_ref if step == steps - 1 else fnext
        turn = 2 * step
        if step > 0:
            sections(source, turn)
            scatter_start(turn)
        collide_levels(source, 0, 8)
        scatter_finish(turn)
        collide_levels(source, 8, LEVELS)
        gather_wait(turn)

        sampled = [[], [], []]
        for s in range(SLOTS):
            wide = jnp.concatenate([window(turn, s, 0), window(turn, s, 1)], axis=1)
            high, low = split(wide)
            both = jnp.concatenate([high, low], axis=0)
            first_part = jnp.dot(both, w_hi[s], preferred_element_type=F32)
            second_part = jnp.dot(high, w_lo[s], preferred_element_type=F32)
            partial = first_part[:48] + first_part[48:] + second_part
            for axis in range(3):
                weighted = partial[axis * LEVELS : (axis + 1) * LEVELS] * up_ref[s]
                sampled[axis].append(jnp.sum(weighted, axis=0, keepdims=True))
        sampled = [jnp.concatenate(rows, axis=0) for rows in sampled]

        if step == 0:
            exchange_wait(bl_tx.at[0], bl_r, "recv")
            bl_rx[me] = bl_tx[me]
            picks = [bl_rx[owners[s], ranks[s]] for s in range(SLOTS)]
            rows = [
                jnp.concatenate([picks[s][k : k + 1] for s in range(SLOTS)], axis=0)
                for k in range(7)
            ]
            area, twist, speed, angle = rows[:4]
            filtered = rows[4:]
            sin_t = jnp.sin(angle)
            cos_t = jnp.cos(angle)
        filtered = [filtered[axis] + MIX * (sampled[axis] - filtered[axis]) for axis in range(3)]
        phase = jnp.concatenate(
            [jnp.full((1, chunk), pp_ref[ids[s], step], jnp.int32) for s in range(SLOTS)], axis=0
        )
        pitch = PITCH_AMP * jnp.sin(2.0 * math.pi * phase.astype(F32) / PHASES)
        axial = filtered[0]
        tangent = speed + sin_t * filtered[1] - cos_t * filtered[2]
        square = axial * axial + tangent * tangent
        magnitude = jnp.sqrt(square)
        sin_p = axial / magnitude
        cos_p = tangent / magnitude
        beta = twist + pitch
        sin_b = jnp.sin(beta)
        cos_b = jnp.cos(beta)
        sin_a = sin_p * cos_b - cos_p * sin_b
        cos_a = cos_p * cos_b + sin_p * sin_b
        lift = 2.0 * math.pi * sin_a * cos_a
        drag = 0.02 + sin_a * sin_a
        dynamic = 0.5 * area * square
        normal = dynamic * (lift * cos_p + drag * sin_p)
        tangential = dynamic * (lift * sin_p - drag * cos_p)
        loads = [normal, -tangential * sin_t, tangential * cos_t]

        turn = 2 * step + 1
        for s in range(SLOTS):
            live = jnp.full((1, chunk), valid[s], jnp.int32) > 0
            weighted = jnp.concatenate(
                [
                    up_ref[s] * jnp.where(live, -SPREAD * loads[axis][s : s + 1], 0.0)
                    for axis in range(3)
                ],
                axis=0,
            )
            high, low = split(weighted)
            both = jnp.concatenate([high, low], axis=0)
            contract = (((1,), (1,)), ((), ()))
            first_part = lax.dot_general(both, w_hi[s], contract, preferred_element_type=F32)
            second_part = lax.dot_general(high, w_lo[s], contract, preferred_element_type=F32)
            section = first_part[:48] + first_part[48:] + second_part
            for half in range(2):
                for block in range(6):
                    at = s * 96 + half * 48 + 8 * block
                    win_tx[turn, at // SHARD, at % SHARD : at % SHARD + 8, :] = section[
                        8 * block : 8 * block + 8, half * CY : half * CY + CY
                    ]
        scatter_start(turn)
        if step == steps - 1:
            for s in range(SLOTS):
                val_ref[s] = jnp.concatenate(
                    [value[s : s + 1] for value in loads + filtered + [phase.astype(F32)] * 2],
                    axis=0,
                )

            def answer(d, carry):
                for e in range(2):
                    total = jnp.zeros((8, chunk), F32)
                    for s in range(SLOTS):
                        mine = valid[s] * (owners[s] == d).astype(jnp.int32)
                        mine = mine * (ranks[s] == e).astype(jnp.int32)
                        total = jnp.where(
                            jnp.full((8, chunk), mine, jnp.int32) > 0, val_ref[s], total
                        )
                    ou_tx[d, e] = total
                return carry

            lax.fori_loop(0, TILES, answer, 0)
        scatter_finish(turn)
        if step == steps - 1:
            exchange_start(lambda to: ou_tx.at[to], ou_rx.at[me], ou_s, ou_r)
        gather_wait(turn)

        forces = []
        for s in range(SLOTS):
            first = jnp.broadcast_to(firsts[s], level_shape)
            halves = [window(turn, s, 0), window(turn, s, 1)]
            forces.append(
                [
                    jnp.where(first == me, halves[0][axis * LEVELS : (axis + 1) * LEVELS], 0.0)
                    + jnp.where(
                        first == me - 1, halves[1][axis * LEVELS : (axis + 1) * LEVELS], 0.0
                    )
                    for axis in range(3)
                ]
            )
        for s in range(SLOTS):
            force = []
            for axis in range(3):
                total = forces[s][axis]
                for other in range(SLOTS):
                    if other != s:
                        same = jnp.full(level_shape, planes[other] - planes[s], jnp.int32) == 0
                        total = total + jnp.where(same, forces[other][axis], 0.0)
                force.append(total)
            out = collide([plane_f[s, q] for q in range(NQ)], force)
            for q in range(NQ):
                plane_p[s, q] = out[q]

        masks = [x_ids == planes[s] for s in range(SLOTS)]

        def settle(z, carry):
            up, down = carry
            for q in range(NQ):
                slab = post[q, z]
                for s in range(SLOTS):
                    slab = jnp.where(masks[s], plane_p[s, q, pl.ds(z, 1), :], slab)
                post[q, z] = slab
                if q in Y_PLUS:
                    lane = Y_PLUS.index(q) * LEVELS + z
                    moved = pltpu.roll(slab, lax.rem(lane + 1, CY), axis=1)
                    up = jnp.where(y_ids == lane, moved, up)
                if q in Y_MINUS:
                    lane = Y_MINUS.index(q) * LEVELS + z
                    down = jnp.where(y_ids == lane, pltpu.roll(slab, lane, axis=1), down)
            return up, down

        nothing = jnp.zeros((CX, CY), F32)
        up, down = lax.fori_loop(0, LEVELS, settle, (nothing, nothing))
        ys_tx[step, 0] = up
        ys_tx[step, 1] = down
        for k, q in enumerate(X_PLUS):
            xs_tx[step, 0, k] = post[q, :, CX - 1, :]
        for k, q in enumerate(X_MINUS):
            xs_tx[step, 1, k] = post[q, :, 0, :]

        def send(src, dst, k, to):
            return pltpu.make_async_remote_copy(
                src_ref=src, dst_ref=dst, send_sem=ha_s.at[step, k], recv_sem=ha_r.at[step, k],
                device_id=to, device_id_type=MESH,
            )

        hops = [
            send(xs_tx.at[step, 0], xs_rx.at[step, 0], 0, {"gx": x_up}),
            send(xs_tx.at[step, 1], xs_rx.at[step, 1], 1, {"gx": x_dn}),
            send(ys_tx.at[step, 0, 8:16], cr_rx.at[step, 0], 4, {"gx": x_up, "gy": y_up}),
            send(ys_tx.at[step, 1, 0:8], cr_rx.at[step, 1], 5, {"gx": x_dn, "gy": y_dn}),
            send(ys_tx.at[step, 1, 8:16], cr_rx.at[step, 2], 6, {"gx": x_up, "gy": y_dn}),
            send(ys_tx.at[step, 0, 0:8], cr_rx.at[step, 3], 7, {"gx": x_dn, "gy": y_up}),
            send(ys_tx.at[step, 0], ys_rx.at[step, 0], 2, {"gy": y_up}),
            send(ys_tx.at[step, 1], ys_rx.at[step, 1], 3, {"gy": y_dn}),
        ]
        for hop in hops:
            hop.start()

        def stream(z, bottom, top):
            for q in range(NQ):
                cx, cy, cz = DIRS[q]
                if (cz == 1 and bottom) or (cz == -1 and top):
                    target[q, z] = post[OPPOSITE[q], z]
                    continue
                slab = post[q, z - cz]
                if cx:
                    slab = pltpu.roll(slab, cx % CX, axis=0)
                if cy:
                    slab = pltpu.roll(slab, cy % CY, axis=1)
                target[q, z] = slab

        stream(0, True, False)
        stream(LEVELS - 1, False, True)

        def stream_body(z, carry):
            stream(z, False, False)
            return carry

        lax.fori_loop(1, LEVELS - 1, stream_body, 0)
        for hop in hops:
            hop.wait_recv()

        packed = {}
        for q in Y_PLUS + Y_MINUS:
            cx, cy, cz = DIRS[q]
            column = ys_rx[step, 0 if cy == 1 else 1]
            if cx:
                corner = {(1, 1): 0, (-1, -1): 1, (1, -1): 2, (-1, 1): 3}[(cx, cy)]
                edge = cr_rx[step, corner, 7:8, :] if cx == 1 else cr_rx[step, corner, 0:1, :]
                column = pltpu.roll(column, cx % CX, axis=0)
                column = jnp.where(x_ids == (0 if cx == 1 else CX - 1), edge, column)
            packed[q] = column

        def edges(z, bottom, top):
            for q in range(NQ):
                cx, cy, cz = DIRS[q]
                if not (cx or cy) or (cz == -1 and bottom) or (cz == 1 and top):
                    continue
                if cx:
                    side, names = (0, X_PLUS) if cx == 1 else (1, X_MINUS)
                    row = xs_rx[step, side, names.index(q), pl.ds(z, 1), :]
                    at = 0 if cx == 1 else CX - 1
                if cx and not cy:
                    target[q, z + cz, at : at + 1, :] = row
                    continue
                slab = target[q, z + cz]
                if cx:
                    row = pltpu.roll(jnp.broadcast_to(row, (8, CY)), cy % CY, axis=1)[0:1]
                    slab = jnp.where(x_ids == at, row, slab)
                names = Y_PLUS if cy == 1 else Y_MINUS
                lane = names.index(q) * LEVELS + z
                to = 0 if cy == 1 else CY - 1
                moved = pltpu.roll(packed[q], lax.rem(to - lane + CY, CY), axis=1)
                target[q, z + cz] = jnp.where(y_ids == to, moved, slab)

        edges(0, True, False)
        edges(LEVELS - 1, False, True)

        def edges_body(z, carry):
            edges(z, False, False)
            return carry

        lax.fori_loop(1, LEVELS - 1, edges_body, 0)
        for hop in hops:
            hop.wait_send()

    exchange_wait(ou_tx.at[0], ou_r, "recv")
    ou_rx[me] = ou_tx[me]

    def place(d, carry):
        lanes = pl.ds(pl.multiple_of(d * chunk, chunk), chunk)
        for e in range(2):
            lo_ref[e, :, lanes] = ou_rx[d, e, 0:3, :]
            io_ref[e, :, lanes] = ou_rx[d, e, 3:6, :]
        return carry

    lax.fori_loop(0, TILES, place, 0)
    exchange_wait(bl_tx.at[0], bl_s, "send")
    exchange_wait(ou_tx.at[0], ou_s, "send")
    for turn in range(2 * steps):
        sends_done(turn)


def local(
    f_in, rotor_place, marker_cell, pitch_phase,
    blade_area, blade_twist, blade_speed, blade_angle, filt_in,
):
    steps = pitch_phase.shape[1]
    owned = filt_in.shape[2]
    markers = filt_in.shape[4]
    chunk = markers // TILES
    turns = 2 * steps
    field = f_in.shape
    vmem = pl.BlockSpec(memory_space=pltpu.VMEM)
    smem = pl.BlockSpec(memory_space=pltpu.SMEM)
    dma = pltpu.SemaphoreType.DMA
    scratch = [
        pltpu.VMEM(field, F32),
        pltpu.VMEM(field, F32),
        pltpu.VMEM((SLOTS, NQ, LEVELS, CY), F32),
        pltpu.VMEM((SLOTS, NQ, LEVELS, CY), F32),
        pltpu.VMEM((turns, REDUCERS, SHARD, CY), F32),
        pltpu.VMEM((turns, TILES, SHARD, CY), F32),
        pltpu.VMEM((turns, REDUCERS, SHARD, CY), F32),
        pltpu.VMEM((TILES, owned, 8, chunk), F32),
        pltpu.VMEM((TILES, owned, 8, chunk), F32),
        pltpu.VMEM((TILES, owned, 8, chunk), F32),
        pltpu.VMEM((TILES, owned, 8, chunk), F32),
        pltpu.VMEM((SLOTS, 2 * CY, chunk), jnp.bfloat16),
        pltpu.VMEM((SLOTS, 2 * CY, chunk), jnp.bfloat16),
        pltpu.VMEM((SLOTS, LEVELS, chunk), F32),
        pltpu.VMEM((SLOTS, 8, chunk), F32),
        pltpu.VMEM((steps, 2, 5, LEVELS, CY), F32),
        pltpu.VMEM((steps, 2, 5, LEVELS, CY), F32),
        pltpu.VMEM((steps, 2, CX, CY), F32),
        pltpu.VMEM((steps, 2, CX, CY), F32),
        pltpu.VMEM((steps, 4, 8, CY), F32),
        dma((turns, TILES)), dma((turns, TILES)), dma((turns, TILES)), dma((turns, TILES)),
        dma((TILES,)), dma((TILES,)), dma((TILES,)), dma((TILES,)),
        dma((steps, 8)), dma((steps, 8)),
    ]
    out = pl.pallas_call(
        mega,
        out_shape=(
            jax.ShapeDtypeStruct(field, F32),
            jax.ShapeDtypeStruct((owned, 3, markers), F32),
            jax.ShapeDtypeStruct((owned, 3, markers), F32),
        ),
        in_specs=[vmem, smem, vmem, smem, vmem, vmem, vmem, vmem, vmem],
        out_specs=(vmem, vmem, vmem),
        scratch_shapes=scratch,
        compiler_params=pltpu.CompilerParams(
            collective_id=0, has_side_effects=True, vmem_limit_bytes=56 * 1024 * 1024
        ),
        name="farm",
    )(
        f_in, rotor_place, marker_cell, pitch_phase,
        blade_area[0, 0], blade_twist[0, 0], blade_speed[0, 0], blade_angle[0, 0], filt_in[0, 0],
    )
    return out[0], out[1][None, None], out[2][None, None]


def solution(mesh):
    blade = P("gx", "gy", None, None)
    marker = P("gx", "gy", None, None, None)
    field = P(None, None, "gx", "gy")
    in_specs = (field, P(), P(), P(), blade, blade, blade, blade, marker)
    out_specs = (field, marker, marker)
    return jax.shard_map(local, mesh=mesh, in_specs=in_specs, out_specs=out_specs, check_vma=False)
```

time: 827 us -> 95.2 us (0.12); the launches traced: 816 us -> 94.9 us
  waiting for transfers between devices: 512 us -> 0 us
  matrix products: 147 us -> 0 us
  Pallas kernels: 0 us -> 82.9 us
  local copies, waits for them, and re-layouts: 67 us -> 11.4 us
  other arithmetic: 52.7 us -> 0 us
  between operations: 22.1 us -> 0.64 us
  starting transfers between devices: 14.8 us -> 0 us
    psum x4 -> x0, waiting for transfers between devices: 494 us -> none  [the longest x2 248 us: local(): sampled = lax.psum(samples, 'gy')]
    dot_general x12 -> x0, matrix products: 147 us -> none  [the longest x6 98 us: sample_section(): jnp.dot(across, flattened, precision=lax.Precision.HIGHEST, preferred_ele...]
    pallas_call x0 -> x1, Pallas kernels: none -> 82.9 us  [local(): pl.pallas_call(mega, out_shape=(jax.ShapeDtypeStruct(field, F32), jax.Sha...]
    slice x14 -> x0, local copies, waits for them, and re-layouts: 27.7 us -> none  [the longest x6 17.4 us: extended(): lax.slice_in_dim(block, 0, width, axis=dim)]
    ppermute x4 -> x0, local copies, waits for them, and re-layouts: 22.8 us -> none  [the longest x2 11.5 us: extended(): lax.ppermute(lax.slice_in_dim(block, 0, width, axis=dim), axis, backward)]
    unnamed x34 -> x0, other arithmetic: 19.7 us -> none
    ppermute x8 -> x0, waiting for transfers between devices: 18.2 us -> none  [the longest x4 11.1 us: extended(): lax.ppermute(lax.slice_in_dim(block, block.shape[dim] - width, None, axis...]
    ppermute x8 -> x0, starting transfers between devices: 14.5 us -> none  [the longest x4 14.1 us: extended(): lax.ppermute(lax.slice_in_dim(block, 0, width, axis=dim), axis, backward)]
  transfers between devices with their start and end apart: 12 -> 0, of which waited for: 10 -> 0; matrix products, arithmetic and copies ran while one was open for 3% -> 0% of each run, Pallas kernels for 0% -> 0%
where the time goes in v1:
time: 95.2 us; the launch traced here: 94.9 us
  Pallas kernels  82.9 us (87%)
  local copies, waits for them, and re-layouts  11.4 us (12%)
    pallas_call x1, Pallas kernels, local(): pl.pallas_call(mega, out_shape=(jax.ShapeDtypeStruct(field, F32), jax.Sha...  82.9 us
    unnamed x6, local copies, waits for them, and re-layouts  11.4 us

profile of v1, /device:TPU:1, one launch (start us, length us, event | category | flops | bytes accessed | tf_op | source)
XLA Modules:
  0.0 94.9 jit_solution(16251073414541206844)
XLA Ops:
  0.6 1.4 %copy.13.rp_ref = s32[40,3]{1,0:T(8,128)} copy(s32[40,3]{0,1:T(4,128)} %param.10) | data formatting | bytes 960 | tf_op args[1]
  2.0 1.4 %copy.14.pp_ref = s32[40,2]{1,0:T(8,128)} copy(s32[40,2]{0,1:T(2,128)} %param.12) | data formatting | bytes 640 | tf_op args[3]
  3.4 1.8 %copy.18 = f32[1,1,2,3,8192]{4,3,2,1,0:T(4,128)} copy(f32[1,1,2,3,8192]{4,2,3,1,0:T(2,128)} %param.17) | data formatting | bytes 393216 | tf_op args[8]
  5.1 82.9 %farm.1 = (f32[19,16,16,128]{3,2,1,0:T(8,128)}, f32[2,3,8192]{2,1,0:T(4,128)}, f32[2,3,8192]{2,1,0:T(4,128)}) custom-call(f32[19,16,16,128]{3,2,1,0:T(8,128)} %f_ref.1, s32[40,3]{1,0:T(8,128)} %copy.13.rp_ref, s32[40,8192]{1,0:T(8,128)} %mc_ref.1, s32[40,2]{1,0:T(8,128)} %copy.14.pp_ref, f32[2,8192]{1,0:T(2,128)} %bitcast.12, f32[2,8192]{1,0:T(2,128)} %bitcast.13, ...), custom_call_target="tpu_custom_call" | custom-call | tf_op jit(solution)/shard_map/farm/pallas_call | solution.py:662
  88.0 1.8 %copy.15 = f32[1,1,2,3,8192]{4,2,3,1,0:T(2,128)} copy(f32[1,1,2,3,8192]{4,3,2,1,0:T(4,128)} %bitcast.11) | data formatting | bytes 393216
  89.8 1.8 %copy.16 = f32[1,1,2,3,8192]{4,2,3,1,0:T(2,128)} copy(f32[1,1,2,3,8192]{4,3,2,1,0:T(4,128)} %bitcast.10) | data formatting | bytes 393216
  91.6 3.4 %copy.20 = f32[19,16,16,128]{3,2,1,0:T(8,128)} copy(f32[19,16,16,128]{3,2,1,0:T(8,128)} %get-tuple-element.15) | data formatting | bytes 4980736
